TPU v7x, 32 devices: a whole 2x2x4 slice. The times are simulated.
32 devices in a mesh: row: 8 (over y, x, core), col: 4 (over z).
Axes of the slice: x: 2, y: 2, z: 4, core: 2. Of those that a mesh axis runs over, the one named last changes fastest.
Arguments:
- covariance: float32 [2, 8192, 8192], P(None, 'row', 'col'), as said below
- forcing: float32 [2, 8192, 8192], P(None, 'row', 'col'), as said below
- coupling: float32 [2, 64, 64], replicated, may hold values from -0.5 to 0.5
- vertical: float32 [2, 128, 128], replicated, may hold values from -0.375 to 0.375
- damping: float32 [64, 128], replicated, may hold values from 0.3 to 3
- advection: float32 [64, 128], replicated, may hold values from -2 to 2
Outputs:
- advanced: float32 [2, 8192, 8192], P(None, 'row', 'col')
Inputs may be any that keep to these rules, and one draw needn't show every extreme that they name: The covariance equals its conjugate transpose: the real plane is symmetric, the imaginary plane antisymmetric. The forcing equals its conjugate transpose: the real plane is symmetric, the imaginary plane antisymmetric.
All inputs are finite; a program needn't handle non-finite values.
Results may differ from a plain program's by a relative error of at most 0.000073.
Values sent between devices are 32-bit elements; how exact they have to be, the bound alone decides.
A program may use at most 320 MiB of HBM per device.

v0:
```python
import jax
import jax.numpy as jnp
from jax import lax
from jax.sharding import PartitionSpec as P

step_size = 0.25


def complex_einsum(pattern, factor, values):

    def single(factor_part, value_part):
        return jnp.einsum(pattern, factor_part, value_part, precision=lax.Precision.HIGHEST)

    real_part = single(factor[0], values[0]) - single(factor[1], values[1])
    imag_part = single(factor[0], values[1]) + single(factor[1], values[0])
    return jnp.stack([real_part, imag_part])


def complex_scale(factor, values):
    real_part = factor[0] * values[0] - factor[1] * values[1]
    imag_part = factor[0] * values[1] + factor[1] * values[0]
    return jnp.stack([real_part, imag_part])


def conjugate(values):
    return jnp.stack([values[0], -values[1]])


def left_apply(by_rows, coupling, vertical, rates):
    total = complex_einsum("lm,amj->alj", vertical, by_rows)
    total = total + complex_einsum("ab,blj->alj", coupling, by_rows)
    return total + complex_scale(rates[:, :, :, None], by_rows)


def right_apply(by_cols, coupling, vertical, rates):
    total = complex_einsum("lm,iam->ial", conjugate(vertical), by_cols)
    total = total + complex_einsum("ab,ibl->ial", conjugate(coupling), by_cols)
    return total + complex_scale(conjugate(rates)[:, None], by_cols)


def tendency(block_tile, forcing, coupling, vertical, rates):
    rows_here = block_tile.shape[1]
    cols_here = block_tile.shape[2]
    levels = vertical.shape[1]
    lats_row = rows_here // levels
    lats_col = cols_here // levels
    by_rows = block_tile.reshape(2, lats_row, levels, cols_here)
    regrouped = lax.all_to_all(by_rows, "row", split_axis=3, concat_axis=1, tiled=True)
    applied = left_apply(regrouped, coupling, vertical, rates)
    left_term = lax.all_to_all(applied, "row", split_axis=1, concat_axis=3, tiled=True)
    left_term = left_term.reshape(2, rows_here, cols_here)
    by_cols = block_tile.reshape(2, rows_here, lats_col, levels)
    regrouped_cols = lax.all_to_all(by_cols, "col", split_axis=1, concat_axis=2, tiled=True)
    applied_cols = right_apply(regrouped_cols, coupling, vertical, rates)
    right_term = lax.all_to_all(
        applied_cols, "col", split_axis=2, concat_axis=1, tiled=True
    ).reshape(2, rows_here, cols_here)
    return left_term + right_term + forcing


def shards(covariance, forcing, coupling, vertical, damping, advection):
    rates = jnp.stack([-damping, advection])
    first_rate = tendency(covariance, forcing, coupling, vertical, rates)
    midpoint = covariance + 0.5 * step_size * first_rate
    return covariance + step_size * tendency(midpoint, forcing, coupling, vertical, rates)


def solution(mesh):
    return jax.shard_map(
        shards,
        mesh=mesh,
        in_specs=(P(None, "row", "col"), P(None, "row", "col"), P(), P(), P(), P()),
        out_specs=P(None, "row", "col"),
        check_vma=False,
    )
```

profile of v0, /device:TPU:0, one launch (start us, length us, event | category | flops | bytes accessed | tf_op | source)
XLA Modules:
  0.0 2441.1 jit_solution(17442187832632348149)
XLA Ops:
  0.0 17.6 copy.149
  39.9 168.1 %all-to-all-done = f32[2,8,128,2048]{2,1,0,3:T(8,128)} async-done(((f32[2,8,128,2048]{2,1,0,3:T(8,128)}), f32[2,8,128,2048]{2,1,0,3:T(8,128)}, u32[]{:S(2)}, u32[]{:S(2)}) %all-to-all-start) | async-done | bytes 16777248 | tf_op jit(solution)/shard_map/all_to_all | solution.py:48
  397.3 19.0 add_bitcast_fusion.4
  439.1 137.1 %all-to-all-done.2 = f32[2,1024,16,128]{3,2,0,1:T(8,128)} async-done(((f32[2,1024,16,128]{3,2,0,1:T(8,128)}), f32[2,1024,16,128]{3,2,0,1:T(8,128)}, u32[]{:S(2)}, u32[]{:S(2)}) %all-to-all-start.2) | async-done | bytes 16777248 | tf_op jit(solution)/shard_map/all_to_all | solution.py:53
  641.2 17.4 fusion.20
  720.1 41.0 %fusion.6 = (f32[1,256,64,128]{3,1,2,0:T(8,128)}, f32[1,256,64,128]{3,1,2,0:T(8,128)}) fusion(f32[256,128,64]{1,2,0:T(8,128)} %fusion.20, f32[256,128,64]{1,2,0:T(8,128)} %fusion.16, f32[256,128,64]{1,2,0:T(8,128)} %fusion.18, f32[256,128,64]{1,2,0:T(8,128)} %fusion.22), kind=kLoop, calls=%fused_computation.16 | loop fusion | flops 4194304 | bytes 50331648 | tf_op jit(solution)/shard_map/stack | solution.py:16
  791.0 17.4 copy.164
  808.4 18.0 reshape.251
  826.3 328.4 %all-to-all-done.3 = f32[2,256,64,128]{3,1,0,2:T(8,128)} async-done(((f32[2,256,64,128]{3,1,0,2:T(8,128)}), f32[2,256,64,128]{3,1,0,2:T(8,128)}, u32[]{:S(2)}, u32[]{:S(2)}) %all-to-all-start.3) | async-done | bytes 16777248 | tf_op jit(solution)/shard_map/all_to_all | solution.py:55
  1154.7 17.8 copy.249
  1172.5 18.0 reshape.253
  1190.4 29.2 %multiply_add_fusion.1 = f32[2,1024,2048]{2,1,0:T(8,128)} fusion(f32[2,1024,2048]{2,1,0:T(8,128)} %param.6, f32[2,1024,2048]{2,1,0:T(8,128)} %param.7, f32[2,1024,2048]{2,1,0:T(8,128)} %reshape.251, f32[2,1024,2048]{2,1,0:T(8,128)} %reshape.253), kind=kLoop, calls=%fused_computation.10 | loop fusion | flops 16777216 | bytes 83886080 | tf_op jit(solution)/shard_map/add | solution.py:64
  1219.6 17.7 copy.181
  1259.5 167.4 %all-to-all-done.4 = f32[2,8,128,2048]{2,1,0,3:T(8,128)} async-done(((f32[2,8,128,2048]{2,1,0,3:T(8,128)}), f32[2,8,128,2048]{2,1,0,3:T(8,128)}, u32[]{:S(2)}, u32[]{:S(2)}) %all-to-all-start.4) | async-done | bytes 16777248 | tf_op jit(solution)/shard_map/all_to_all | solution.py:48
  1659.0 135.3 %all-to-all-done.6 = f32[2,1024,16,128]{3,2,0,1:T(8,128)} async-done(((f32[2,1024,16,128]{3,2,0,1:T(8,128)}), f32[2,1024,16,128]{3,2,0,1:T(8,128)}, u32[]{:S(2)}, u32[]{:S(2)}) %all-to-all-start.6) | async-done | bytes 16777248 | tf_op jit(solution)/shard_map/all_to_all | solution.py:53
  1845.3 17.4 fusion.12
  1934.3 18.2 fusion.5
  1952.6 18.4 fusion.4
  2012.2 17.4 copy.196
  2029.6 18.0 reshape.255
  2047.5 328.4 %all-to-all-done.7 = f32[2,256,64,128]{3,1,0,2:T(8,128)} async-done(((f32[2,256,64,128]{3,1,0,2:T(8,128)}), f32[2,256,64,128]{3,1,0,2:T(8,128)}, u32[]{:S(2)}, u32[]{:S(2)}) %all-to-all-start.7) | async-done | bytes 16777248 | tf_op jit(solution)/shard_map/all_to_all | solution.py:55
  2375.9 17.8 copy.212
  2393.7 18.0 reshape.257
  2411.7 29.2 %multiply_add_fusion = f32[2,1024,2048]{2,1,0:T(8,128)} fusion(f32[2,1024,2048]{2,1,0:T(8,128)} %param.6, f32[2,1024,2048]{2,1,0:T(8,128)} %param.7, f32[2,1024,2048]{2,1,0:T(8,128)} %reshape.255, f32[2,1024,2048]{2,1,0:T(8,128)} %reshape.257), kind=kLoop, calls=%fused_computation.9 | loop fusion | flops 16777216 | bytes 83886080 | tf_op jit(solution)/shard_map/add | solution.py:65
  (136 shorter events, 808.5 us)
Async XLA Ops:
  17.6 190.4 %all-to-all-start = ((f32[2,8,128,2048]{2,1,0,3:T(8,128)}), f32[2,8,128,2048]{2,1,0,3:T(8,128)}, u32[]{:S(2)}, u32[]{:S(2)}) async-start(f32[2,8,128,2048]{2,1,0,3:T(8,128)} %copy.149), calls=%async_computation | async-start | bytes 33554432 | tf_op jit(solution)/shard_map/all_to_all | solution.py:48
  39.9 175.3 %copy-start.13 = (f32[64,128]{1,0:T(8,128)S(1)}, f32[64,128]{1,0:T(8,128)}, u32[]{:S(2)}) copy-start(f32[64,128]{1,0:T(8,128)} %param.10) | copy-start | bytes 98308
  208.0 368.2 %all-to-all-start.2 = ((f32[2,1024,16,128]{3,2,0,1:T(8,128)}), f32[2,1024,16,128]{3,2,0,1:T(8,128)}, u32[]{:S(2)}, u32[]{:S(2)}) async-start(f32[2,1024,16,128]{3,2,0,1:T(8,128)} %copy.213), calls=%async_computation.2 | async-start | bytes 33554432 | tf_op jit(solution)/shard_map/all_to_all | solution.py:53
  215.2 497.9 %copy-start.7 = (f32[64,128]{1,0:T(8,128)}, f32[64,128]{1,0:T(8,128)S(1)}, u32[]{:S(2)}) copy-start(f32[64,128]{1,0:T(8,128)S(1)} %neg.27) | copy-start | bytes 98308
  349.3 20.4 slice-start.6
  349.3 31.2 %slice-start.4 = ((s8[8388608]{0:T(1024)(128)(4,1)}), s8[4194304]{0:T(1024)(128)(4,1)S(1)}, s32[]{:S(2)}) async-start(s8[8388608]{0:T(1024)(128)(4,1)} %bitcast.244), calls=%async_computation.12 | async-start | bytes 8388608
  360.4 20.2 slice-start.5
  380.6 9.6 copy-start.9
  576.2 207.7 %all-to-all-start.1 = ((f32[2,64,128,256]{2,3,0,1:T(8,128)}), f32[2,64,128,256]{2,3,0,1:T(8,128)}, u32[]{:S(2)}, u32[]{:S(2)}) async-start(f32[2,64,128,256]{2,3,0,1:T(8,128)} %copy.163), calls=%async_computation.1 | async-start | bytes 33554432 | tf_op jit(solution)/shard_map/all_to_all | solution.py:50
  582.2 130.9 %copy-start.11 = (f32[64,128]{1,0:T(8,128)}, f32[64,128]{1,0:T(8,128)S(1)}, u32[]{:S(2)}) copy-start(f32[64,128]{1,0:T(8,128)S(1)} %neg.32) | copy-start | bytes 98308
  784.0 370.8 %all-to-all-start.3 = ((f32[2,256,64,128]{3,1,0,2:T(8,128)}), f32[2,256,64,128]{3,1,0,2:T(8,128)}, u32[]{:S(2)}, u32[]{:S(2)}) async-start(f32[2,256,64,128]{3,1,0,2:T(8,128)} %copy.179), calls=%async_computation.3 | async-start | bytes 33554432 | tf_op jit(solution)/shard_map/all_to_all | solution.py:55
  1237.3 189.7 %all-to-all-start.4 = ((f32[2,8,128,2048]{2,1,0,3:T(8,128)}), f32[2,8,128,2048]{2,1,0,3:T(8,128)}, u32[]{:S(2)}, u32[]{:S(2)}) async-start(f32[2,8,128,2048]{2,1,0,3:T(8,128)} %copy.181), calls=%async_computation.4 | async-start | bytes 33554432 | tf_op jit(solution)/shard_map/all_to_all | solution.py:48
  1426.9 367.4 %all-to-all-start.6 = ((f32[2,1024,16,128]{3,2,0,1:T(8,128)}), f32[2,1024,16,128]{3,2,0,1:T(8,128)}, u32[]{:S(2)}, u32[]{:S(2)}) async-start(f32[2,1024,16,128]{3,2,0,1:T(8,128)} %copy.197), calls=%async_computation.6 | async-start | bytes 33554432 | tf_op jit(solution)/shard_map/all_to_all | solution.py:53
  1565.3 18.7 slice-start.2
  1565.3 27.8 %slice-start = ((s8[8388608]{0:T(1024)(128)(4,1)}), s8[4194304]{0:T(1024)(128)(4,1)S(1)}, s32[]{:S(2)}) async-start(s8[8388608]{0:T(1024)(128)(4,1)} %bitcast.233), calls=%async_computation.8 | async-start | bytes 8388608
  1574.7 9.4 slice-start.3
  1574.7 18.5 slice-start.1
  1613.6 11.3 copy-start.8
  1613.6 11.3 copy-start.10
  1794.3 210.6 %all-to-all-start.5 = ((f32[2,64,128,256]{2,3,0,1:T(8,128)}), f32[2,64,128,256]{2,3,0,1:T(8,128)}, u32[]{:S(2)}, u32[]{:S(2)}) async-start(f32[2,64,128,256]{2,3,0,1:T(8,128)} %copy.195), calls=%async_computation.5 | async-start | bytes 33554432 | tf_op jit(solution)/shard_map/all_to_all | solution.py:50
  1819.1 106.0 %copy-start = (f32[1,256,4,16,128]{4,1,3,2,0:T(8,128)}, f32[1,256,4,16,128]{4,1,3,2,0:T(8,128)S(1)}, u32[]{:S(2)}) copy-start(f32[1,256,4,16,128]{4,1,3,2,0:T(8,128)S(1)} %copy.199) | copy-start | bytes 25165828
  1828.1 86.1 %copy-start.1 = (f32[1,256,4,16,128]{4,1,3,2,0:T(8,128)}, f32[1,256,4,16,128]{4,1,3,2,0:T(8,128)S(1)}, u32[]{:S(2)}) copy-start(f32[1,256,4,16,128]{4,1,3,2,0:T(8,128)S(1)} %copy.200) | copy-start | bytes 25165828
  1952.6 18.4 copy-start.12
  2004.9 371.0 %all-to-all-start.7 = ((f32[2,256,64,128]{3,1,0,2:T(8,128)}), f32[2,256,64,128]{3,1,0,2:T(8,128)}, u32[]{:S(2)}, u32[]{:S(2)}) async-start(f32[2,256,64,128]{3,1,0,2:T(8,128)} %copy.211), calls=%async_computation.7 | async-start | bytes 33554432 | tf_op jit(solution)/shard_map/all_to_all | solution.py:55
  (6 other events, 54.1 us)
where the time goes:
time: 2450 us; the launch traced here: 2440 us
  waiting for transfers between devices  1260 us (51%)
  local copies, waits for them, and re-layouts  457 us (19%)
  matrix products  386 us (16%)
  other arithmetic  281 us (11%)
  starting transfers between devices  52 us (2%)
    all_to_all x2, waiting for transfers between devices, tendency(): lax.all_to_all(applied_cols, 'col', split_axis=2, concat_axis=1, tiled=True)  657 us
    dot_general x32, matrix products, single(): jnp.einsum(pattern, factor_part, value_part, precision=lax.Precision.HIGH...  386 us
    all_to_all x2, waiting for transfers between devices, tendency(): lax.all_to_all(by_rows, 'row', split_axis=3, concat_axis=1, tiled=True)  336 us
    all_to_all x2, waiting for transfers between devices, tendency(): lax.all_to_all(by_cols, 'col', split_axis=1, concat_axis=2, tiled=True)  272 us
    another operation x6, other arithmetic, complex_einsum(): return jnp.stack([real_part, imag_part])  119 us
    slice x12, local copies, waits for them, and re-layouts, complex_einsum(): real_part = single(factor[0], values[0]) - single(factor[1], values[1])  79.4 us
    dot_general x8, local copies, waits for them, and re-layouts, single(): jnp.einsum(pattern, factor_part, value_part, precision=lax.Precision.HIGH...  74.2 us
  transfers between devices with their start and end apart: 8, of which 6 were waited for; matrix products, arithmetic and copies ran while one was open for 39% of the time, Pallas kernels for 0%

commit v1 on v0

v1 whole, which is shorter than its diff:
```python
import jax
import jax.numpy as jnp
from jax import lax
from jax.sharding import PartitionSpec as P

step_size = 0.25


def real_form(matrix):
    re, im = matrix
    top = jnp.stack([re, -im], axis=-2)
    bottom = jnp.stack([im, re], axis=-2)
    return jnp.stack([top, bottom], axis=-4)


def shards(row_size, col_size, covariance, forcing, coupling, vertical, damping, advection):
    rows_here, cols_here = covariance.shape[1:]
    lats, levels = damping.shape
    lats_row = rows_here // levels
    groups = cols_here // rows_here
    width = rows_here // row_size
    cols = groups * width

    eye = jnp.eye(levels, dtype=jnp.float32)
    level_op = real_form(
        (
            vertical[0] - damping[:, :, None] * eye,
            vertical[1] + advection[:, :, None] * eye,
        )
    ).reshape(lats, 2 * levels, 2 * levels)
    lat_op = jnp.moveaxis(real_form(coupling), (0, 1, 2, 3), (1, 0, 3, 2)).reshape(2 * lats, 2 * lats)

    def to_columns(tile):
        split = tile.reshape(2, lats_row, levels, groups, row_size, width)
        split = split.transpose(4, 1, 0, 2, 3, 5).reshape(row_size * lats_row, 2, levels, cols)
        return lax.all_to_all(split, "row", split_axis=0, concat_axis=0, tiled=True)

    def to_tile(block):
        parts = lax.all_to_all(block, "row", split_axis=0, concat_axis=0, tiled=True)
        parts = parts.reshape(row_size, lats_row, 2, levels, groups, width)
        return parts.transpose(2, 1, 3, 4, 0, 5).reshape(2, rows_here, cols_here)

    def left(block):
        by_level = jnp.einsum(
            "axy,ayj->axj",
            level_op,
            block.reshape(lats, 2 * levels, cols),
            precision=lax.Precision.HIGH,
        ).reshape(block.shape)
        by_lat = jnp.einsum(
            "xy,ylj->xlj",
            lat_op,
            block.reshape(2 * lats, levels, cols),
            precision=lax.Precision.HIGH,
        ).reshape(block.shape)
        return by_level + by_lat

    def adjoint(block):
        planes = block.transpose(1, 0, 2, 3).reshape(2, col_size, groups, row_size, width, cols)
        send = planes.transpose(1, 3, 0, 5, 2, 4).reshape(col_size * row_size, 2, cols, cols)
        got = lax.all_to_all(send, ("col", "row"), split_axis=0, concat_axis=0, tiled=True)
        got = got.reshape(col_size, row_size, 2, groups, width, cols)
        got = got.transpose(2, 0, 3, 1, 4, 5).reshape(2, lats, levels, cols)
        return jnp.stack([got[0], -got[1]], axis=1)

    cov = to_columns(covariance)
    force = to_columns(forcing)
    first = left(cov)
    midpoint = cov + (0.5 * step_size) * (first + adjoint(first) + force)
    second = left(midpoint)
    return to_tile(cov + step_size * (second + adjoint(second) + force))


def solution(mesh):
    row_size, col_size = mesh.shape["row"], mesh.shape["col"]

    def body(*args):
        return shards(row_size, col_size, *args)

    return jax.shard_map(
        body,
        mesh=mesh,
        in_specs=(P(None, "row", "col"), P(None, "row", "col"), P(), P(), P(), P()),
        out_specs=P(None, "row", "col"),
        check_vma=False,
    )
```

time: 2450 us -> 1740 us (0.71)
  waiting for transfers between devices: 1260 us -> 591 us
  blocking collectives: 0 us -> 554 us
  matrix products: 386 us -> 110 us
  other arithmetic: 281 us -> 132 us
  local copies, waits for them, and re-layouts: 457 us -> 334 us
  starting transfers between devices: 52 us -> 16.7 us
    all_to_all x8 -> x3, waiting for transfers between devices: 1260 us -> 591 us  [the longest x1 328 us: adjoint(): lax.all_to_all(send, ('col', 'row'), split_axis=0, concat_axis=0, tiled=T...]
    all_to_all x0 -> x2, blocking collectives: none -> 554 us  [the longest x1 366 us: adjoint(): lax.all_to_all(send, ('col', 'row'), split_axis=0, concat_axis=0, tiled=T...]
    dot_general x32 -> x4, matrix products: 386 us -> 110 us  [the longest x2 67.3 us: left(): jnp.einsum('xy,ylj->xlj', lat_op, block.reshape(2 * lats, levels, cols),...]
    another operation x6 -> x3, other arithmetic: 119 us -> 23.6 us  [real_form(): return jnp.stack([top, bottom], axis=-4)]
    dot_general x8 -> x0, local copies, waits for them, and re-layouts: 74.2 us -> none  [single(): jnp.einsum(pattern, factor_part, value_part, precision=lax.Precision.HIGH...]
    slice x12 -> x2, local copies, waits for them, and re-layouts: 79.4 us -> 16.4 us  [adjoint(): return jnp.stack([got[0], -got[1]], axis=1)]
    all_to_all x8 -> x3, local copies, waits for them, and re-layouts: 102 us -> 47.7 us  [the longest x2 34.9 us: adjoint(): lax.all_to_all(send, ('col', 'row'), split_axis=0, concat_axis=0, tiled=T...]
    add x6 -> x2, other arithmetic: 125 us -> 71.1 us  [the longest x1 35.6 us: shards(): return to_tile(cov + step_size * (second + adjoint(second) + force))]
  transfers between devices with their start and end apart: 8 -> 3, of which waited for: 6 -> 3; matrix products, arithmetic and copies ran while one was open for 39% -> 9% of each run, Pallas kernels for 0% -> 0%
where the time goes in v1:
time: 1740 us
  waiting for transfers between devices  591 us (34%)
  blocking collectives  554 us (32%)
  local copies, waits for them, and re-layouts  334 us (19%)
  other arithmetic  132 us (8%)
  matrix products  110 us (6%)
    all_to_all x1, blocking collectives, adjoint(): lax.all_to_all(send, ('col', 'row'), split_axis=0, concat_axis=0, tiled=T...  366 us
    all_to_all x1, waiting for transfers between devices, adjoint(): lax.all_to_all(send, ('col', 'row'), split_axis=0, concat_axis=0, tiled=T...  328 us
    all_to_all x2, waiting for transfers between devices, to_columns(): return lax.all_to_all(split, 'row', split_axis=0, concat_axis=0, tiled=True)  263 us
    all_to_all x1, blocking collectives, to_tile(): lax.all_to_all(block, 'row', split_axis=0, concat_axis=0, tiled=True)  188 us
    dot_general x2, matrix products, left(): jnp.einsum('xy,ylj->xlj', lat_op, block.reshape(2 * lats, levels, cols),...  67.3 us
    reshape x2, local copies, waits for them, and re-layouts, to_columns(): split.transpose(4, 1, 0, 2, 3, 5)  49.8 us
    dot_general x2, matrix products, left(): jnp.einsum('axy,ayj->axj', level_op, block.reshape(lats, 2 * levels, cols...  42.5 us
    add x1, other arithmetic, shards(): return to_tile(cov + step_size * (second + adjoint(second) + force))  35.6 us
  transfers between devices with their start and end apart: 3, of which 3 were waited for; matrix products, arithmetic and copies ran while one was open for 9% of the time, Pallas kernels for 0%

profile of v1, /device:TPU:0, one launch (start us, length us, event | category | flops | bytes accessed | tf_op | source)
XLA Modules:
  0.0 1737.6 jit_solution(15273670187505201565)
XLA Ops:
  19.5 24.9 %reshape.128 = f32[64,2,128,256]{3,1,2,0:T(2,128)} reshape(f32[8,8,2,128,2,128]{5,4,2,3,1,0:T(2,128)} %bitcast.106) | data formatting | bytes 33554432 | tf_op jit(solution)/shard_map/reshape | solution.py:35
  50.6 19.9 %fusion.20 = (f32[64,128,1,128]{3,2,1,0:T(1,128)S(1)}, f32[64,128,1,128]{3,2,1,0:T(1,128)S(1)}, f32[64,128,1,128]{3,2,1,0:T(1,128)S(1)}) fusion(f32[128,128]{1,0:T(8,128)S(1)} %fusion.16, f32[64,128]{1,0:T(8,128)S(1)} %copy-done.2, f32[128,128]{1,0:T(8,128)S(1)} %get-tuple-element.13, f32[64,128]{1,0:T(8,128)S(1)} %copy-done.3, ...), kind=kLoop, calls=%fused_computation.37 | loop fusion | flops 5242880 | bytes 12845056 | tf_op jit(solution)/shard_map/neg | solution.py:11
  94.1 21.6 %reshape.129 = f32[64,256,256]{2,1,0:T(8,128)} reshape(f32[64,2,128,2,128]{4,3,2,1,0:T(2,128)} %pad_maximum_fusion) | data formatting | bytes 33554432 | tf_op jit(solution)/shard_map/reshape | solution.py:30
  115.7 119.3 %all-to-all-done = f32[64,2,128,256]{3,1,2,0:T(2,128)} async-done(((f32[64,2,128,256]{3,1,2,0:T(2,128)}), f32[64,2,128,256]{3,1,2,0:T(2,128)}, u32[]{:S(2)}, u32[]{:S(2)}) %all-to-all-start) | async-done | bytes 16777248 | tf_op jit(solution)/shard_map/all_to_all | solution.py:36
  247.9 21.2 %fusion.23 = f32[64,256,256]{2,1,0:T(8,128)} fusion(f32[64,256,256]{2,1,0:T(8,128)} %reshape.129, f32[64,256,256]{2,1,0:T(8,128)} %bitcast.102), kind=kOutput, calls=%fused_computation.40 | convolution fusion | flops 6442450944 | bytes 50331648 | tf_op jit(solution)/shard_map/axy,ayj->axj/dot_general | solution.py:44
  269.1 39.6 %bitcast_add_fusion.1 = f32[64,2,128,256]{3,0,2,1:T(8,128)} fusion(f32[64,2,128,256]{3,2,1,0:T(8,128)} %bitcast.100, f32[64,2,128,256]{3,1,2,0:T(2,128)} %all-to-all-done, f32[1,64,2,64]{3,1,2,0:T(8,128)S(1)} %get-tuple-element.19, f32[1,64,2,64]{3,1,2,0:T(8,128)S(1)} %get-tuple-element.18), kind=kOutput, calls=%fused_computation.12 | convolution fusion | flops 3225436160 | bytes 50397184 | tf_op jit(solution)/shard_map/xy,ylj->xlj/dot_general | solution.py:50
  308.7 17.8 %copy.38 = f32[2,4,2,8,128,256]{5,4,2,0,3,1:T(8,128)} copy(f32[2,4,2,8,128,256]{5,3,2,1,4,0:T(8,128)} %bitcast.97) | data formatting | bytes 33554432 | tf_op jit(solution)/shard_map/reshape | solution.py:59
  351.0 24.9 %reshape.136 = f32[64,2,128,256]{3,1,2,0:T(2,128)} reshape(f32[8,8,2,128,2,128]{5,4,2,3,1,0:T(2,128)} %bitcast.107) | data formatting | bytes 33554432 | tf_op jit(solution)/shard_map/reshape | solution.py:35
  375.9 328.1 %all-to-all-done.1 = f32[32,2,256,256]{2,3,1,0:T(8,128)} async-done(((f32[32,2,256,256]{2,3,1,0:T(8,128)}), f32[32,2,256,256]{2,3,1,0:T(8,128)}, u32[]{:S(2)}, u32[]{:S(2)}) %all-to-all-start.1) | async-done | bytes 16777248 | tf_op jit(solution)/shard_map/all_to_all | solution.py:61
  709.8 17.5 %copy.39 = f32[32,2,256,256]{3,2,1,0:T(8,128)} copy(f32[32,2,256,256]{2,3,1,0:T(8,128)} %all-to-all-done.1) | data formatting | bytes 33554432 | tf_op jit(solution)/shard_map/all_to_all | solution.py:61
  750.0 143.7 %all-to-all-done.2 = f32[64,2,128,256]{3,1,2,0:T(2,128)} async-done(((f32[64,2,128,256]{3,1,2,0:T(2,128)}), f32[64,2,128,256]{3,1,2,0:T(2,128)}, u32[]{:S(2)}, u32[]{:S(2)}) %all-to-all-start.2) | async-done | bytes 16777248 | tf_op jit(solution)/shard_map/all_to_all | solution.py:36
  893.7 35.5 %fusion.2 = f32[64,2,128,256]{3,0,2,1:T(8,128)} fusion(f32[64,2,128,256]{3,0,2,1:T(8,128)} %bitcast_add_fusion.1, f32[64,1,128,256]{3,0,2,1:T(8,128)} %bitcast.113, f32[64,1,128,256]{3,0,2,1:T(8,128)} %bitcast.112, f32[64,2,128,256]{3,1,2,0:T(2,128)} %all-to-all-done, f32[64,2,128,256]{3,1,2,0:T(2,128)} %all-to-all-done.2), kind=kLoop, calls=%fused_computation.4 | loop fusion | flops 20971520 | bytes 83886080 | tf_op jit(solution)/shard_map/add | solution.py:69
  929.2 17.8 %copy.45 = f32[64,2,128,256]{3,2,1,0:T(8,128)} copy(f32[64,2,128,256]{3,0,2,1:T(8,128)} %fusion.2) | data formatting | bytes 33554432 | tf_op jit(solution)/shard_map/add | solution.py:69
  947.0 21.3 %fusion.24 = f32[64,256,256]{2,1,0:T(8,128)} fusion(f32[64,256,256]{2,1,0:T(8,128)} %reshape.129, f32[64,256,256]{2,1,0:T(8,128)} %bitcast.101), kind=kOutput, calls=%fused_computation.41 | convolution fusion | flops 6442450944 | bytes 50331648 | tf_op jit(solution)/shard_map/axy,ayj->axj/dot_general | solution.py:44
  968.4 27.7 %bitcast_add_fusion = f32[64,2,128,256]{3,0,2,1:T(8,128)} fusion(f32[64,2,128,256]{3,2,1,0:T(8,128)} %bitcast.99, f32[64,2,128,256]{3,0,2,1:T(8,128)} %fusion.2, f32[1,64,2,64]{3,1,2,0:T(8,128)S(1)} %get-tuple-element.19, f32[1,64,2,64]{3,1,2,0:T(8,128)S(1)} %get-tuple-element.18), kind=kOutput, calls=%fused_computation.9 | convolution fusion | flops 3225436160 | bytes 50397184 | tf_op jit(solution)/shard_map/xy,ylj->xlj/dot_general | solution.py:50
  996.1 15.6 copy.48
  1011.7 365.8 %all_to_all.25 = f32[32,2,256,256]{2,3,1,0:T(8,128)} all-to-all(f32[32,2,256,256]{2,3,1,0:T(8,128)S(1)} %bitcast.111), channel_id=1, replica_groups=mesh['row'=8,'col'=4] {'col','row'}, dimensions={0} | all-to-all | bytes 33554432 | tf_op jit(solution)/shard_map/all_to_all | solution.py:61
  1377.6 17.4 %copy.49 = f32[32,2,256,256]{3,2,1,0:T(8,128)} copy(f32[32,2,256,256]{2,3,1,0:T(8,128)} %all_to_all.25) | data formatting | bytes 33554432 | tf_op jit(solution)/shard_map/all_to_all | solution.py:61
  1425.7 35.6 %fusion.5 = f32[64,2,128,256]{3,0,2,1:T(8,128)} fusion(f32[64,2,128,256]{3,0,2,1:T(8,128)} %bitcast_add_fusion, f32[64,1,128,256]{3,0,2,1:T(8,128)} %bitcast.115, f32[64,1,128,256]{3,0,2,1:T(8,128)S(1)} %bitcast.114, f32[64,2,128,256]{3,1,2,0:T(2,128)} %all-to-all-done, f32[64,2,128,256]{3,1,2,0:T(2,128)} %all-to-all-done.2), kind=kLoop, calls=%fused_computation.8 | loop fusion | flops 20971520 | bytes 83886080 | tf_op jit(solution)/shard_map/add | solution.py:71
  1461.2 27.7 %copy.54 = f32[64,2,128,256]{3,1,2,0:T(2,128)S(1)} copy(f32[64,2,128,256]{3,0,2,1:T(8,128)} %fusion.5) | data formatting | bytes 33554432 | tf_op jit(solution)/shard_map/add | solution.py:71
  1489.0 187.9 %all_to_all.26 = f32[64,2,128,256]{3,1,2,0:T(2,128)} all-to-all(f32[64,2,128,256]{3,1,2,0:T(2,128)S(1)} %copy.54), channel_id=1, replica_groups=mesh['row'=8,'col'=4] {'row'}, dimensions={0} | all-to-all | bytes 33554432 | tf_op jit(solution)/shard_map/all_to_all | solution.py:39
  1676.9 24.9 %reshape.142 = f32[8,8,2,128,2,128]{5,4,2,3,1,0:T(2,128)} reshape(f32[64,2,128,256]{3,1,2,0:T(2,128)} %all_to_all.26) | data formatting | bytes 33554432 | tf_op jit(solution)/shard_map/reshape | solution.py:40
  1701.7 17.7 %copy.55 = f32[2,8,128,2,8,128]{5,4,3,2,1,0:T(8,128)} copy(f32[2,8,128,2,8,128]{5,3,0,2,1,4:T(2,128)} %bitcast.108) | data formatting | bytes 33554432 | tf_op jit(solution)/shard_map/transpose | solution.py:41
  1719.4 18.0 %reshape.143 = f32[2,1024,2048]{2,1,0:T(8,128)} reshape(f32[2,8,128,2,8,128]{5,4,3,2,1,0:T(8,128)} %copy.55) | data formatting | bytes 33554432 | tf_op jit(solution)/shard_map/reshape | solution.py:41
  (29 shorter events, 145.7 us)
Async XLA Ops:
  44.4 6.1 copy-start.1
  44.4 6.1 copy-start.2
  44.4 6.1 copy-start.3
  44.4 190.7 %all-to-all-start = ((f32[64,2,128,256]{3,1,2,0:T(2,128)}), f32[64,2,128,256]{3,1,2,0:T(2,128)}, u32[]{:S(2)}, u32[]{:S(2)}) async-start(f32[64,2,128,256]{3,1,2,0:T(2,128)} %reshape.128), calls=%async_computation | async-start | bytes 33554432 | tf_op jit(solution)/shard_map/all_to_all | solution.py:36
  94.1 21.6 %copy-start = (f32[2,64,64]{2,1,0:T(8,128)S(1)}, f32[2,64,64]{2,1,0:T(8,128)}, u32[]{:S(2)}) copy-start(f32[2,64,64]{2,1,0:T(8,128)} %param.8) | copy-start | bytes 98308
  326.5 377.5 %all-to-all-start.1 = ((f32[32,2,256,256]{2,3,1,0:T(8,128)}), f32[32,2,256,256]{2,3,1,0:T(8,128)}, u32[]{:S(2)}, u32[]{:S(2)}) async-start(f32[32,2,256,256]{2,3,1,0:T(8,128)} %bitcast.103), calls=%async_computation.1 | async-start | bytes 33554432 | tf_op jit(solution)/shard_map/all_to_all | solution.py:61
  704.0 189.7 %all-to-all-start.2 = ((f32[64,2,128,256]{3,1,2,0:T(2,128)}), f32[64,2,128,256]{3,1,2,0:T(2,128)}, u32[]{:S(2)}, u32[]{:S(2)}) async-start(f32[64,2,128,256]{3,1,2,0:T(2,128)} %reshape.136), calls=%async_computation.2 | async-start | bytes 33554432 | tf_op jit(solution)/shard_map/all_to_all | solution.py:36
